TPU v7x, 128 devices: a whole 4x4x4 slice. The times are simulated.
128 devices in a mesh: row: 8 (over x, core), col: 16 (over y, z).
Axes of the slice: x: 4, y: 4, z: 4, core: 2. Of those that a mesh axis runs over, the one named last changes fastest.
Arguments:
- valence: bfloat16 [2, 16, 32768], replicated, may hold values from -6 to 6
- conduction: bfloat16 [2, 128, 32768], replicated, may hold values from -6 to 6
- valence_energy: float32 [16], replicated, may hold values from -8 to -1
- conduction_energy: float32 [128], replicated, may hold values from 0.5 to 6
- band_pairs: int32 [1024, 2], P(('row', 'col')), may hold values from 0 to 127, as said below
- grid_index: int32 [16384], replicated, may hold values from 0 to 32767, as said below
Outputs:
- response: float32 [2, 16384, 16384], P(None, 'row', 'col')
Inputs may be any that keep to these rules, and one draw needn't show every extreme that they name: `band_pairs`: the rows are distinct combinations of a valence band below 16 and a conduction band below 128, half of all combinations. `grid_index`: the 16384 entries are distinct.
All inputs are finite; a program needn't handle non-finite values.
Results may differ from a plain program's by a relative error of at most 0.0039.
Values may be sent and summed in bfloat16 or wider, within the bound.
A program may use at most 192 MiB of HBM per device.

v0:
```python
import math
import jax
import jax.numpy as jnp
from jax import lax
from jax.sharding import PartitionSpec as P

N1 = 32
N2 = 32
N3 = 32
NVB = 16
NCB = 128


def tables(length):
    position = jnp.arange(length, dtype=jnp.int32)
    phase_angle = (position[:, None] * position[None, :] % length).astype(jnp.float32) * (
        2.0 * math.pi / length
    )
    return (jnp.cos(phase_angle), jnp.sin(phase_angle))


def plane_table():
    plane_size = N2 * N3
    position = jnp.arange(plane_size, dtype=jnp.int32)
    second = position // N3
    third = position % N3
    phase_index = (
        second[:, None] * second[None, :] % N2 * N3 + third[:, None] * third[None, :] % N3 * N2
    )
    phase_angle = (phase_index % plane_size).astype(jnp.float32) * (2.0 * math.pi / plane_size)
    cosine = jnp.cos(phase_angle)
    sine_table = jnp.sin(phase_angle)
    upper = jnp.concatenate([cosine, -sine_table], axis=1)
    lower = jnp.concatenate([sine_table, cosine], axis=1)
    return jnp.concatenate([upper, lower], axis=0)


def transform(rho_real, rho_imag):
    pair_count = rho_real.shape[0]
    plane_size = N2 * N3
    stacked = jnp.concatenate(
        [
            rho_real.reshape(pair_count, N1, plane_size),
            rho_imag.reshape(pair_count, N1, plane_size),
        ],
        axis=2,
    )
    plane = jnp.dot(
        stacked.reshape(pair_count * N1, 2 * plane_size),
        plane_table(),
        precision=lax.Precision.HIGHEST,
    )
    plane = plane.reshape(pair_count, N1, 2 * plane_size)
    cosine, sine_table = tables(N1)
    cos_part = jnp.einsum("kr,prx->pkx", cosine, plane, precision=lax.Precision.HIGHEST)
    sin_part = jnp.einsum("kr,prx->pkx", sine_table, plane, precision=lax.Precision.HIGHEST)
    out_real = cos_part[:, :, :plane_size] + sin_part[:, :, plane_size:]
    out_imag = cos_part[:, :, plane_size:] - sin_part[:, :, :plane_size]
    return (out_real.reshape(pair_count, -1), out_imag.reshape(pair_count, -1))


def pair_spectrum(valence, conduction, valence_energy, conduction_energy, band_pairs):
    valence_rows = jnp.take(valence, band_pairs[:, 0], axis=1).astype(jnp.float32)
    conduction_rows = jnp.take(conduction, band_pairs[:, 1], axis=1).astype(jnp.float32)
    rho_real = valence_rows[0] * conduction_rows[0] + valence_rows[1] * conduction_rows[1]
    rho_imag = valence_rows[0] * conduction_rows[1] - valence_rows[1] * conduction_rows[0]
    out_real, out_imag = transform(rho_real, rho_imag)
    normalize = 1.0 / math.sqrt(N1 * N2 * N3)
    spectrum = jnp.stack([out_real, out_imag]) * normalize
    valence_hot = (
        band_pairs[:, 0][:, None] == jnp.arange(valence_energy.shape[0], dtype=jnp.int32)[None, :]
    )
    conduction_hot = (
        band_pairs[:, 1][:, None]
        == jnp.arange(conduction_energy.shape[0], dtype=jnp.int32)[None, :]
    )
    energy_gap = jnp.sum(jnp.where(valence_hot, valence_energy[None, :], 0.0), axis=1) - jnp.sum(
        jnp.where(conduction_hot, conduction_energy[None, :], 0.0), axis=1
    )
    weights = 2.0 / (math.sqrt(NVB * NCB // 2) * energy_gap)
    return (spectrum, weights)


def contract(weighted_part, operand, left_dims, right_dims):
    full_left = (0,) + tuple((d + 1 for d in left_dims))
    full_right = (0,) + tuple((d + 1 for d in right_dims))
    real_part = lax.dot_general(
        weighted_part,
        operand,
        ((full_left, full_right), ((), ())),
        preferred_element_type=jnp.float32,
    )
    pair_dims = ((left_dims, right_dims), ((), ()))
    imag_part = lax.dot_general(
        weighted_part[0], operand[1], pair_dims, preferred_element_type=jnp.float32
    ) - lax.dot_general(weighted_part[1], operand[0], pair_dims, preferred_element_type=jnp.float32)
    return jnp.stack([real_part, imag_part])


def body(valence, conduction, valence_energy, conduction_energy, band_pairs, grid_index):
    spectrum, weights = pair_spectrum(
        valence, conduction, valence_energy, conduction_energy, band_pairs
    )
    row_count = lax.axis_size("row")
    column_count = lax.axis_size("col")
    selected = jnp.take(spectrum, grid_index, axis=2)
    weighted = (weights[None, :, None] * selected).astype(jnp.bfloat16)
    density = selected.astype(jnp.bfloat16)
    weighted_block = lax.all_to_all(weighted, "row", split_axis=2, concat_axis=1, tiled=True)
    density_block = lax.all_to_all(density, "col", split_axis=2, concat_axis=1, tiled=True)
    weighted_all = lax.all_gather(weighted_block, "col", axis=1, tiled=True)
    density_all = lax.all_gather(density_block, "row", axis=1, tiled=True)
    pair_count = density_all.shape[1]
    per_device = pair_count // (row_count * column_count)
    weighted_split = weighted_all.reshape(
        2, column_count, row_count, per_device, weighted_all.shape[2]
    )
    density_split = density_all.reshape(
        2, row_count, column_count, per_device, density_all.shape[2]
    )
    return contract(weighted_split, density_split, (0, 1, 2), (1, 0, 2))


def solution(mesh):
    return jax.shard_map(
        body,
        mesh=mesh,
        in_specs=(P(), P(), P(), P(), P(("row", "col"), None), P()),
        out_specs=P(None, "row", "col"),
        check_vma=False,
    )
```

profile of v0, /device:TPU:1, one launch (start us, length us, event | category | flops | bytes accessed | tf_op | source)
XLA Modules:
  0.0 724.0 jit_solution(14251131210681987142)
XLA Ops:
  6.5 0.0 all-gather.5.cloned.1.call-start
  6.5 0.8 fusion.55
  7.4 0.8 and_bitcast_fusion.1
  8.2 3.6 gather_fusion.1
  11.8 1.5 convert_bitcast_fusion.1
  13.3 0.0 copy-done
  13.3 3.5 gather_fusion
  16.9 0.0 copy-start.2
  16.9 0.2 convert_bitcast_fusion.2
  17.1 1.4 copy-done.2
  18.4 0.3 multiply_add_fusion
  18.8 0.6 copy.50
  19.4 0.6 copy.51
  20.0 23.7 %fusion.25 = (f32[1024,1024]{1,0:T(8,128)}, f32[1024,1024]{1,0:T(8,128)}, f32[1024,1024]{1,0:T(8,128)}) fusion(s32[1024]{0:T(1024)S(1)} %get-tuple-element.24, s32[1024]{0:T(1024)S(1)} %get-tuple-element.25), kind=kLoop, calls=%fused_computation.53 | loop fusion | flops 41943040 | bytes 12591104 | tf_op jit(solution)/shard_map/neg | solution.py:33
  43.7 22.3 %fusion = f32[8,32,2048]{2,1,0:T(8,128)} fusion(f32[1024,1024]{1,0:T(8,128)} %get-tuple-element.15, f32[1024,1024]{1,0:T(8,128)} %get-tuple-element.14, f32[1024,1024]{1,0:T(8,128)} %get-tuple-element.13, f32[8,32,1024]{2,1,0:T(8,128)S(1)} %bitcast.102, f32[8,32,1024]{2,1,0:T(8,128)S(1)} %bitcast.103), kind=kOutput, calls=%fused_computation.4 | convolution fusion | flops 12898009088 | bytes 16777216 | tf_op jit(solution)/shard_map/dot_general | solution.py:48
  66.0 3.8 convolution_bitcast_fusion.1
  69.9 2.1 convolution_bitcast_fusion.2
  72.0 1.4 slice_add_fusion
  73.4 2.4 stack_reshape.6
  75.8 1.2 stack_reshape.7
  77.0 1.7 maximum_multiply_fusion
  78.7 28.8 %copy.31 = f32[2,8,32768]{1,0,2:T(2,128)} copy(f32[2,8,32768]{2,1,0:T(8,128)S(1)} %maximum_multiply_fusion) | data formatting | bytes 4194304 | tf_op jit(solution)/shard_map/mul | solution.py:69
  107.5 251.9 %gather_fusion.2 = f32[16384,2,8]{2,1,0:T(2,128)} fusion(f32[2,8,32768]{1,0,2:T(2,128)} %copy.31, s32[16384]{0:T(1024)S(1)} %fusion.26), kind=kCustom, calls=%fused_computation.2 | custom fusion | bytes 2162688 | tf_op jit(solution)/shard_map/jit(_take)/gather | solution.py:106
  359.4 71.1 %fusion.59 = bf16[16384,2,8]{2,1,0:T(2,128)(2,1)} fusion(f32[16384,2,8]{2,1,0:T(2,128)} %gather_fusion.2, pred[16384]{0:T(1024)(128)(4,1)S(1)} %compare_and_fusion), kind=kLoop, calls=%fused_computation.113 | loop fusion | flops 262144 | bytes 1589248
  430.5 10.5 %reshape.154 = bf16[16,2,8192]{2,1,0:T(2,128)(2,1)S(1)} reshape(bf16[16384,2,8]{2,1,0:T(2,128)(2,1)} %fusion.59) | data formatting | bytes 1048576
  440.9 18.7 %all_to_all.36 = bf16[16,2,8192]{2,1,0:T(2,128)(2,1)S(1)} all-to-all(bf16[16,2,8192]{2,1,0:T(2,128)(2,1)S(1)} %reshape.154), channel_id=1, replica_groups=mesh['row'=8,'col'=16] {'col'}, dimensions={0} | all-to-all | bytes 1048576 | tf_op jit(solution)/shard_map/all_to_all | solution.py:110
  459.6 10.9 %reshape.155 = bf16[16384,2,8]{2,1,0:T(2,128)(2,1)} reshape(bf16[16,2,8192]{2,1,0:T(2,128)(2,1)S(1)} %all_to_all.36) | data formatting | bytes 1048576
  470.6 19.3 %copy.33 = bf16[2,16,8,1024]{3,2,1,0:T(8,128)(2,1)} copy(bf16[2,16,8,1024]{2,0,3,1:T(2,128)(2,1)} %bitcast.90) | data formatting | bytes 1048576 | tf_op jit(solution)/shard_map/all_to_all | solution.py:110
  489.8 0.0 all-gather.5.cloned.1.call-update
  489.8 0.0 all-gather.3.cloned.1.call-start
  489.9 0.2 select_reduce_fusion
  490.1 0.2 select_reduce_fusion.1
  490.3 59.2 %fusion.60 = bf16[16384,2,8]{2,1,0:T(2,128)(2,1)} fusion(f32[16384,2,8]{2,1,0:T(2,128)} %gather_fusion.2, pred[16384]{0:T(1024)(128)(4,1)S(1)} %compare_and_fusion, f32[8]{0:T(128)S(1)} %multiply_divide_fusion), kind=kLoop, calls=%fused_computation.114 | loop fusion | flops 786432 | bytes 1589280
  549.4 10.4 %reshape.152 = bf16[8,2,16384]{2,1,0:T(2,128)(2,1)S(1)} reshape(bf16[16384,2,8]{2,1,0:T(2,128)(2,1)} %fusion.60) | data formatting | bytes 1048576
  559.9 15.6 %all_to_all.37 = bf16[8,2,16384]{2,1,0:T(2,128)(2,1)S(1)} all-to-all(bf16[8,2,16384]{2,1,0:T(2,128)(2,1)S(1)} %reshape.152), channel_id=1, replica_groups=mesh['row'=8,'col'=16] {'row'}, dimensions={0} | all-to-all | bytes 1048576 | tf_op jit(solution)/shard_map/all_to_all | solution.py:109
  575.5 10.9 %reshape.153 = bf16[16384,2,8]{2,1,0:T(2,128)(2,1)} reshape(bf16[8,2,16384]{2,1,0:T(2,128)(2,1)S(1)} %all_to_all.37) | data formatting | bytes 1048576
  586.3 19.2 %copy.32 = bf16[2,8,8,2048]{3,2,1,0:T(8,128)(2,1)} copy(bf16[2,8,8,2048]{2,0,3,1:T(2,128)(2,1)} %bitcast.91) | data formatting | bytes 1048576 | tf_op jit(solution)/shard_map/all_to_all | solution.py:109
  605.5 0.0 all-gather.3.cloned.1.call-update
  605.5 0.0 all-gather.5.cloned.1.call-done
  605.6 4.7 fusion.58
  610.2 62.7 %all-gather.3.cloned.1.call-done = bf16[2,1024,2048]{2,1,0:T(8,128)(2,1)} async-done(((bf16[2,64,2048]{2,1,0:T(8,128)(2,1)}), bf16[2,1024,2048]{2,1,0:T(8,128)(2,1)}) %all-gather.3.cloned.1.call-update) | async-done | bytes 8388624 | tf_op jit(solution)/shard_map/all_gather | solution.py:111
  672.9 14.5 %convolution_bitcast_fusion = f32[1,2048,1024]{2,1,0:T(8,128)} fusion(bf16[2,16,8,8,2048]{4,3,2,1,0:T(8,128)(2,1)} %bitcast.92, bf16[2,8,16,8,1024]{4,3,2,1,0:T(8,128)(2,1)} %bitcast.93), kind=kOutput, calls=%fused_computation.31 | convolution fusion | flops 8589934592 | bytes 20971520 | tf_op jit(solution)/shard_map/dot_general | solution.py:87
  687.4 5.4 fusion.57
  692.8 0.0 copy-done.6
  692.8 6.9 fusion.21
  699.8 7.4 %fusion.8 = f32[1,2048,1024]{2,1,0:T(8,128)S(1)} fusion(f32[2048,1024,1,1]{1,0,3,2:T(8,128)} %fusion.21, bf16[16,8,8,2048]{3,2,1,0:T(8,128)(2,1)S(1)} %bitcast.96, bf16[8,16,8,1024]{3,2,1,0:T(8,128)(2,1)S(1)} %bitcast.100), kind=kOutput, calls=%fused_computation.16 | convolution fusion | flops 4297064448 | bytes 23068672 | tf_op jit(solution)/shard_map/dot_general | solution.py:96
  707.1 0.0 copy-start.1
  707.2 10.0 %pad_maximum_fusion = f32[2,2048,1024]{2,1,0:T(8,128)} fusion(f32[1,2048,1024]{2,1,0:T(8,128)S(1)} %fusion.8, f32[1,2048,1024]{2,1,0:T(8,128)} %convolution_bitcast_fusion), kind=kLoop, calls=%fused_computation.11 | loop fusion | flops 4194304 | bytes 33554432 | tf_op jit(solution)/shard_map/stack | solution.py:97
  (20 shorter events, 0.1 us)
Async XLA Ops:
  6.5 6.8 copy-start
  6.5 599.0 %all-gather.5.cloned.1.call-start = ((), (), s32[]{:S(2)}) async-start(), calls=%async_computation.3 | async-start | bytes 4718592 | tf_op jit(solution)/shard_map/all_gather | solution.py:112
  16.9 1.6 copy-start.2
  66.0 3.8 copy-start.3
  66.0 6.0 copy-start.7
  470.6 19.3 %copy-start.8 = (f32[128]{0:T(128)S(1)}, f32[128]{0:T(128)}, u32[]{:S(2)}) copy-start(f32[128]{0:T(128)} %param.9) | copy-start | bytes 1540
  470.6 19.5 %copy-start.9 = (f32[16]{0:T(128)S(1)}, f32[16]{0:T(128)}, u32[]{:S(2)}) copy-start(f32[16]{0:T(128)} %param.8) | copy-start | bytes 196
  489.8 183.1 %all-gather.3.cloned.1.call-start = ((), (), s32[]{:S(2)}) async-start(), calls=%async_computation.2 | async-start | bytes 8912896 | tf_op jit(solution)/shard_map/all_gather | solution.py:111
  687.4 5.4 copy-start.6
  692.8 7.0 copy-start.4
  692.8 7.0 copy-start.5
  707.1 10.0 %copy-start.1 = (bf16[2,16,32768]{2,1,0:T(8,128)(2,1)S(1)}, bf16[2,16,32768]{2,1,0:T(8,128)(2,1)}, u32[]{:S(2)}) copy-start(bf16[2,16,32768]{2,1,0:T(8,128)(2,1)} %param.6) | copy-start | bytes 6291460
Sparse Core Ops, SparseCore 0:
  490.0 31.7 all-gather.4
  605.7 67.1 all-gather.2
where the time goes:
time: 734 us; the launch traced here: 724 us
  local copies, waits for them, and re-layouts  385 us (52%)
  other arithmetic  171 us (23%)
  waiting for transfers between devices  62.7 us (9%)
  matrix products  57 us (8%)
  blocking collectives  34.3 us (5%)
  between operations  13.6 us (2%)
    gather x1, local copies, waits for them, and re-layouts, body(): selected = jnp.take(spectrum, grid_index, axis=2)  252 us
    unnamed x2, other arithmetic  130 us
    all_gather x1, waiting for transfers between devices, body(): weighted_all = lax.all_gather(weighted_block, 'col', axis=1, tiled=True)  62.7 us
    unnamed x26, local copies, waits for them, and re-layouts  45.3 us
    mul x1, local copies, waits for them, and re-layouts, pair_spectrum(): spectrum = jnp.stack([out_real, out_imag]) * normalize  28.8 us
    neg x1, other arithmetic, plane_table(): upper = jnp.concatenate([cosine, -sine_table], axis=1)  23.7 us
    dot_general x1, matrix products, transform(): jnp.dot(stacked.reshape(pair_count * N1, 2 * plane_size), plane_table(),...  22.3 us
    all_to_all x1, local copies, waits for them, and re-layouts, body(): lax.all_to_all(density, 'col', split_axis=2, concat_axis=1, tiled=True)  19.3 us
  transfers between devices with their start and end apart: 2, of which 1 were waited for; matrix products, arithmetic and copies ran while one was open for 14% of the time, Pallas kernels for 0%

commit v1 on v0

--- a/solution.py
+++ b/solution.py
@@ -108,7 +108,9 @@
     density = selected.astype(jnp.bfloat16)
     weighted_block = lax.all_to_all(weighted, "row", split_axis=2, concat_axis=1, tiled=True)
     density_block = lax.all_to_all(density, "col", split_axis=2, concat_axis=1, tiled=True)
-    weighted_all = lax.all_gather(weighted_block, "col", axis=1, tiled=True)
+    weighted_all = jnp.concatenate(
+        lax.all_to_all(jnp.stack([weighted_block] * lax.axis_size("col")), "col", 0, 0), axis=1
+    )
     density_all = lax.all_gather(density_block, "row", axis=1, tiled=True)
     pair_count = density_all.shape[1]
     per_device = pair_count // (row_count * column_count)

time: 734 us -> 789 us (1.075)
  waiting for transfers between devices: 62.7 us -> 111 us
  blocking collectives: 34.3 us -> 0 us
  local copies, waits for them, and re-layouts: 385 us -> 406 us
  starting transfers between devices: 0.04 us -> 20.3 us
    all_to_all x0 -> x3, waiting for transfers between devices: none -> 76.5 us  [the longest x1 76.5 us: body(): lax.all_to_all(jnp.stack([weighted_block] * lax.axis_size('col')), 'col',...]
    all_gather x1 -> x0, waiting for transfers between devices: 62.7 us -> none  [body(): weighted_all = lax.all_gather(weighted_block, 'col', axis=1, tiled=True)]
    all_gather x1, waiting for transfers between devices: 0.02 us -> 34.8 us  [body(): density_all = lax.all_gather(density_block, 'row', axis=1, tiled=True)]
    all_to_all x2 -> x0, blocking collectives: 34.3 us -> none  [the longest x1 18.7 us: body(): lax.all_to_all(density, 'col', split_axis=2, concat_axis=1, tiled=True)]
    all_to_all x0 -> x3, starting transfers between devices: none -> 20.3 us  [the longest x1 7.77 us: body(): lax.all_to_all(density, 'col', split_axis=2, concat_axis=1, tiled=True)]
    reshape x0 -> x1, local copies, waits for them, and re-layouts: none -> 11.4 us  [body(): jnp.concatenate(lax.all_to_all(jnp.stack([weighted_block] * lax.axis_size...]
    unnamed x26 -> x34, local copies, waits for them, and re-layouts: 45.3 us -> 46.8 us
    unnamed x2 -> x3, other arithmetic: 130 us -> 131 us
  transfers between devices with their start and end apart: 2 -> 4, of which waited for: 1 -> 2; matrix products, arithmetic and copies ran while one was open for 14% -> 17% of each run, Pallas kernels for 0% -> 0%
where the time goes in v1:
time: 789 us; the launch traced here: 778 us
  local copies, waits for them, and re-layouts  406 us (51%)
  other arithmetic  168 us (21%)
  waiting for transfers between devices  111 us (14%)
  matrix products  57.7 us (7%)
  starting transfers between devices  20.3 us (3%)
  between operations  14 us (2%)
    gather x1, local copies, waits for them, and re-layouts, body(): selected = jnp.take(spectrum, grid_index, axis=2)  252 us
    unnamed x3, other arithmetic  131 us
    all_to_all x1, waiting for transfers between devices, body(): lax.all_to_all(jnp.stack([weighted_block] * lax.axis_size('col')), 'col',...  76.5 us
    unnamed x34, local copies, waits for them, and re-layouts  46.8 us
    all_gather x1, waiting for transfers between devices, body(): density_all = lax.all_gather(density_block, 'row', axis=1, tiled=True)  34.8 us
    mul x1, local copies, waits for them, and re-layouts, pair_spectrum(): spectrum = jnp.stack([out_real, out_imag]) * normalize  29 us
    neg x1, other arithmetic, plane_table(): upper = jnp.concatenate([cosine, -sine_table], axis=1)  23.7 us
    dot_general x1, matrix products, transform(): jnp.dot(stacked.reshape(pair_count * N1, 2 * plane_size), plane_table(),...  22.3 us
  transfers between devices with their start and end apart: 4, of which 2 were waited for; matrix products, arithmetic and copies ran while one was open for 17% of the time, Pallas kernels for 0%

profile of v1, /device:TPU:1, one launch (start us, length us, event | category | flops | bytes accessed | tf_op | source)
XLA Modules:
  0.0 777.7 jit_solution(13077495643563549349)
XLA Ops:
  6.5 0.8 fusion.55
  7.4 0.8 and_bitcast_fusion.1
  8.2 3.6 gather_fusion.1
  11.8 1.5 convert_bitcast_fusion.1
  13.3 3.5 gather_fusion
  16.9 0.2 convert_bitcast_fusion.2
  17.1 1.4 copy-done.2
  18.4 0.3 multiply_add_fusion
  18.8 0.6 copy.62
  19.4 0.6 copy.63
  20.0 23.7 %fusion.25 = (f32[1024,1024]{1,0:T(8,128)}, f32[1024,1024]{1,0:T(8,128)}, f32[1024,1024]{1,0:T(8,128)}) fusion(s32[1024]{0:T(1024)S(1)} %get-tuple-element.24, s32[1024]{0:T(1024)S(1)} %get-tuple-element.25), kind=kLoop, calls=%fused_computation.53 | loop fusion | flops 41943040 | bytes 12591104 | tf_op jit(solution)/shard_map/neg | solution.py:33
  43.7 22.3 %fusion = f32[8,32,2048]{2,1,0:T(8,128)} fusion(f32[1024,1024]{1,0:T(8,128)} %get-tuple-element.15, f32[1024,1024]{1,0:T(8,128)} %get-tuple-element.14, f32[1024,1024]{1,0:T(8,128)} %get-tuple-element.13, f32[8,32,1024]{2,1,0:T(8,128)S(1)} %bitcast.105, f32[8,32,1024]{2,1,0:T(8,128)S(1)} %bitcast.106), kind=kOutput, calls=%fused_computation.4 | convolution fusion | flops 12898009088 | bytes 16777216 | tf_op jit(solution)/shard_map/dot_general | solution.py:48
  66.0 3.8 convolution_bitcast_fusion.1
  69.8 2.1 convolution_bitcast_fusion.2
  72.0 1.4 slice_add_fusion
  73.3 2.4 stack_reshape.6
  75.8 1.2 stack_reshape.7
  76.9 1.7 maximum_multiply_fusion
  78.7 29.0 %copy.40 = f32[2,8,32768]{1,0,2:T(2,128)} copy(f32[2,8,32768]{2,1,0:T(8,128)S(1)} %maximum_multiply_fusion) | data formatting | bytes 4194304 | tf_op jit(solution)/shard_map/mul | solution.py:69
  107.6 252.1 %gather_fusion.2 = f32[16384,2,8]{2,1,0:T(2,128)} fusion(f32[2,8,32768]{1,0,2:T(2,128)} %copy.40, s32[16384]{0:T(1024)S(1)} %fusion.26), kind=kCustom, calls=%fused_computation.2 | custom fusion | bytes 2162688 | tf_op jit(solution)/shard_map/jit(_take)/gather | solution.py:106
  359.7 0.2 select_reduce_fusion
  359.9 0.2 select_reduce_fusion.1
  360.1 71.7 %fusion.60 = bf16[16384,2,8]{2,1,0:T(2,128)(2,1)} fusion(f32[16384,2,8]{2,1,0:T(2,128)} %gather_fusion.2, pred[16384]{0:T(1024)(128)(4,1)S(1)} %compare_and_fusion, f32[8]{0:T(128)S(1)} %multiply_divide_fusion), kind=kLoop, calls=%fused_computation.114 | loop fusion | flops 786432 | bytes 1589280
  431.8 11.2 %reshape.155 = bf16[8,2,16384]{2,1,0:T(2,128)(2,1)} reshape(bf16[16384,2,8]{2,1,0:T(2,128)(2,1)} %fusion.60) | data formatting | bytes 1048576
  443.0 5.8 all-to-all-start
  448.8 59.1 %fusion.59 = bf16[16384,2,8]{2,1,0:T(2,128)(2,1)} fusion(f32[16384,2,8]{2,1,0:T(2,128)} %gather_fusion.2, pred[16384]{0:T(1024)(128)(4,1)S(1)} %compare_and_fusion), kind=kLoop, calls=%fused_computation.113 | loop fusion | flops 262144 | bytes 1589248
  507.9 11.2 %reshape.157 = bf16[16,2,8192]{2,1,0:T(2,128)(2,1)} reshape(bf16[16384,2,8]{2,1,0:T(2,128)(2,1)} %fusion.59) | data formatting | bytes 1048576
  519.1 7.8 all-to-all-start.2
  526.8 10.9 %reshape.156 = bf16[16384,2,8]{2,1,0:T(2,128)(2,1)} reshape(bf16[8,2,16384]{2,1,0:T(2,128)(2,1)S(1)} %all-to-all-done) | data formatting | bytes 1048576
  537.7 17.7 %copy.41 = bf16[2,8,8,2048]{3,1,2,0:T(8,128)(2,1)S(1)} copy(bf16[2,8,8,2048]{1,0,3,2:T(2,128)(2,1)} %bitcast.91) | data formatting | bytes 1048576 | tf_op jit(solution)/shard_map/all_to_all | solution.py:109
  555.4 4.5 stack.14
  559.9 6.7 all-to-all-start.1
  566.6 0.0 all-gather.2.cloned.1.call-start
  566.6 10.9 %reshape.158 = bf16[16384,2,8]{2,1,0:T(2,128)(2,1)} reshape(bf16[16,2,8192]{2,1,0:T(2,128)(2,1)S(1)} %all-to-all-done.2) | data formatting | bytes 1048576
  577.5 19.2 %copy.43 = bf16[2,16,8,1024]{3,2,1,0:T(8,128)(2,1)} copy(bf16[2,16,8,1024]{2,0,3,1:T(2,128)(2,1)} %bitcast.92) | data formatting | bytes 1048576 | tf_op jit(solution)/shard_map/all_to_all | solution.py:110
  596.7 0.0 all-gather.2.cloned.1.call-update
  596.7 34.8 %all-gather.2.cloned.1.call-done = bf16[2,1024,1024]{2,1,0:T(8,128)(2,1)} async-done(((bf16[2,128,1024]{2,1,0:T(8,128)(2,1)}), bf16[2,1024,1024]{2,1,0:T(8,128)(2,1)}) %all-gather.2.cloned.1.call-update) | async-done | bytes 4194320 | tf_op jit(solution)/shard_map/all_gather | solution.py:114
  631.5 4.6 fusion.58
  636.1 76.5 %all-to-all-done.1 = bf16[16,2,64,2048]{3,2,1,0:T(8,128)(2,1)} async-done(((bf16[16,2,64,2048]{3,2,1,0:T(8,128)(2,1)}), bf16[16,2,64,2048]{3,2,1,0:T(8,128)(2,1)}, u32[]{:S(2)}, u32[]{:S(2)}) %all-to-all-start.1) | async-done | bytes 8388640 | tf_op jit(solution)/shard_map/all_to_all | solution.py:112
  712.7 11.4 %copy.42 = bf16[2,16,64,2048]{3,1,2,0:T(8,128)(2,1)} copy(bf16[2,16,64,2048]{3,2,0,1:T(8,128)(2,1)} %bitcast.17) | data formatting | bytes 16777216 | tf_op jit(solution)/shard_map/reshape | solution.py:111
  724.1 3.8 fusion.57
  727.9 0.0 slice-start
  727.9 2.3 copy.45
  730.2 4.2 copy.47
  734.5 12.4 %convolution_bitcast_fusion = f32[1,2048,1024]{2,1,0:T(8,128)} fusion(bf16[2,16,8,8,2048]{4,1,3,2,0:T(8,128)(2,1)S(1)} %bitcast.95, bf16[2,8,16,8,1024]{4,3,2,1,0:T(8,128)(2,1)S(1)} %bitcast.96), kind=kOutput, calls=%fused_computation.31 | convolution fusion | flops 8589934592 | bytes 20971520 | tf_op jit(solution)/shard_map/dot_general | solution.py:87
  746.9 7.3 fusion.21
  754.2 9.8 %fusion.8 = f32[1,2048,1024]{2,1,0:T(8,128)S(1)} fusion(f32[2048,1024,1,1]{1,0,3,2:T(8,128)} %fusion.21, bf16[16,8,8,2048]{3,0,2,1:T(8,128)(2,1)S(1)} %bitcast.97, bf16[8,16,8,1024]{3,2,1,0:T(8,128)(2,1)S(1)} %bitcast.103), kind=kOutput, calls=%fused_computation.16 | convolution fusion | flops 4297064448 | bytes 23068672 | tf_op jit(solution)/shard_map/dot_general | solution.py:96
  764.1 6.4 pad_maximum_fusion
  (34 shorter events, 0.1 us)
Async XLA Ops:
  6.5 6.8 copy-start
  16.9 1.6 copy-start.2
  66.0 3.8 copy-start.3
  66.0 5.9 copy-start.9
  78.7 281.0 %copy-start.10 = (f32[128]{0:T(128)S(1)}, f32[128]{0:T(128)}, u32[]{:S(2)}) copy-start(f32[128]{0:T(128)} %param.9) | copy-start | bytes 1540
  78.7 281.2 %copy-start.11 = (f32[16]{0:T(128)S(1)}, f32[16]{0:T(128)}, u32[]{:S(2)}) copy-start(f32[16]{0:T(128)} %param.8) | copy-start | bytes 196
  443.0 76.1 %all-to-all-start = ((bf16[8,2,16384]{2,1,0:T(2,128)(2,1)}), bf16[8,2,16384]{2,1,0:T(2,128)(2,1)S(1)}, u32[]{:S(2)}, u32[]{:S(2)}) async-start(bf16[8,2,16384]{2,1,0:T(2,128)(2,1)} %reshape.155), calls=%async_computation | async-start | bytes 1048576 | tf_op jit(solution)/shard_map/all_to_all | solution.py:109
  519.1 36.3 %all-to-all-start.2 = ((bf16[16,2,8192]{2,1,0:T(2,128)(2,1)}), bf16[16,2,8192]{2,1,0:T(2,128)(2,1)S(1)}, u32[]{:S(2)}, u32[]{:S(2)}) async-start(bf16[16,2,8192]{2,1,0:T(2,128)(2,1)} %reshape.157), calls=%async_computation.2 | async-start | bytes 1048576 | tf_op jit(solution)/shard_map/all_to_all | solution.py:110
  559.9 152.8 %all-to-all-start.1 = ((bf16[16,2,64,2048]{3,2,1,0:T(8,128)(2,1)}), bf16[16,2,64,2048]{3,2,1,0:T(8,128)(2,1)}, u32[]{:S(2)}, u32[]{:S(2)}) async-start(bf16[16,2,64,2048]{3,2,1,0:T(8,128)(2,1)} %stack.14), calls=%async_computation.1 | async-start | bytes 16777216 | tf_op jit(solution)/shard_map/all_to_all | solution.py:112
  566.6 65.0 %all-gather.2.cloned.1.call-start = ((), (), s32[]{:S(2)}) async-start(), calls=%async_computation.3 | async-start | bytes 4718592 | tf_op jit(solution)/shard_map/all_gather | solution.py:114
  727.9 6.6 slice-start
  730.2 4.3 slice-start.1
  730.2 4.3 copy-start.5
  734.5 12.4 %copy-start.8 = (bf16[1,1024,1024]{2,1,0:T(8,128)(2,1)S(1)}, bf16[1,1024,1024]{2,1,0:T(8,128)(2,1)}, u32[]{:S(2)}) copy-start(bf16[1,1024,1024]{2,1,0:T(8,128)(2,1)} %get-tuple-element.8) | copy-start | bytes 6291460
  746.9 7.3 copy-start.6
  746.9 7.3 copy-start.7
  754.2 9.8 %copy-start.4 = (f32[1,2048,1024]{2,1,0:T(8,128)S(1)}, f32[1,2048,1024]{2,1,0:T(8,128)}, u32[]{:S(2)}) copy-start(f32[1,2048,1024]{2,1,0:T(8,128)} %convolution_bitcast_fusion) | copy-start | bytes 25165828
  764.1 6.5 copy-start.1
Sparse Core Ops, SparseCore 0:
  596.8 34.6 all-gather.1
